TPU v7x, 32 devices: a whole 2x2x4 slice. The times are simulated.
32 devices in a mesh: grp: 16 (over z, x, core), mem: 2 (over y).
Axes of the slice: x: 2, y: 2, z: 4, core: 2. Of those that a mesh axis runs over, the one named last changes fastest.
Arguments:
- forcing: float32 [16, 256, 32, 128], P(None, 'grp', 'mem'), may hold values from -8 to 8
- aggregate: int32 [64, 8, 32], P('grp', 'mem'), may hold values from 0 to 8191, as said below
- factors: float32 [64, 128, 128], P('mem'), may hold values from -1.5 to 1.5, as said below
Outputs:
- solution: float32 [16, 256, 32, 128], P(None, 'grp', 'mem')
Inputs may be any that keep to these rules, and one draw needn't show every extreme that they name: Coarse unknowns are numbered over the fine blocks with the first block index taken modulo half the number of blocks along the first dimension, consecutive numbers lying close together in the other dimensions, so that an aggregate joins blocks of both halves of the grid; a few blocks take the entry of a block beside them. `factors`: each of the 64 blocks is lower triangular with its diagonal between 0.5 and 1.5.
All inputs are finite; a program needn't handle non-finite values.
Results may differ from a plain program's by a relative error of at most 0.00013.
Values sent between devices are 32-bit elements; how exact they have to be, the bound alone decides.
A program may use at most 128 MiB of HBM per device.

v0:
```python
import jax
import jax.numpy as jnp
from jax import lax
from jax.sharding import PartitionSpec as P

NC = 8192
PRE = 3
POST = 2
relaxation = 0.8


def with_halo(cells, sides, width):
    for axis, dim in sides:
        count = lax.axis_size(axis)
        ends = count - 1
        head = lax.slice_in_dim(cells, 0, width, axis=dim)
        tail = lax.slice_in_dim(cells, cells.shape[dim] - width, cells.shape[dim], axis=dim)
        cells = jnp.concatenate(
            [
                lax.ppermute(tail, axis, [(i, (i + 1) % count) for i in range(ends)]),
                cells,
                lax.ppermute(head, axis, [((i + 1) % count, i) for i in range(ends)]),
            ],
            axis=dim,
        )
    return cells


def stencil_inner(padded):
    centre = padded[:, 1:-1, 1:-1]
    beside = padded[:, 2:, 1:-1] + padded[:, :-2, 1:-1]
    beside = beside + padded[:, 1:-1, 2:] + padded[:, 1:-1, :-2]
    zeros_face = jnp.zeros(centre.shape[:3] + (1,), centre.dtype)
    upper_z = jnp.concatenate([centre[..., 1:], zeros_face], axis=3)
    lower_z = jnp.concatenate([zeros_face, centre[..., :-1]], axis=3)
    return 6.0 * centre - (beside + upper_z + lower_z)


def apply_operator(values):
    padded = with_halo(values, (("grp", 1), ("mem", 2)), 1)
    return stencil_inner(padded)


def restrict_blocks(residual, aggregate):
    blk_x, blk_y, blk_z = aggregate.shape
    sides = residual.shape[0]
    means = (
        residual.reshape(sides, blk_x, 4, blk_y, 4, blk_z, 4)
        .mean(axis=(2, 4, 6))
        .reshape(sides, -1)
    )
    summed = jax.ops.segment_sum(means.T, aggregate.reshape(-1), num_segments=NC)
    return summed.T


def prolong_blocks(coarse_fix, ids, valid):
    blk_x, blk_y, blk_z = ids.shape
    sides = coarse_fix.shape[0]
    picked = jnp.take(coarse_fix, ids.reshape(-1), axis=1) * valid.reshape(1, -1)
    picked = picked.reshape(sides, blk_x, 1, blk_y, 1, blk_z, 1)
    spread = jnp.broadcast_to(picked, (sides, blk_x, 4, blk_y, 4, blk_z, 4))
    return spread.reshape(sides, blk_x * 4, blk_y * 4, blk_z * 4)


def solve_blocks(coarse_rhs, factors):
    block_count = factors.shape[0]
    block_size = factors.shape[1]
    sides = coarse_rhs.shape[0]
    blocks = coarse_rhs.reshape(sides, block_count, block_size)
    inner = jnp.einsum("kbj,bij->kbi", blocks, factors, precision=lax.Precision.HIGHEST)
    result = jnp.einsum("kbi,bij->kbj", inner, factors, precision=lax.Precision.HIGHEST)
    return result.reshape(sides, block_count * block_size)


def shards(forcing, aggregate, factors):
    weight = relaxation / 6.0
    smoothed = weight * forcing
    for repeat in range(PRE - 1):
        smoothed = smoothed + weight * (forcing - apply_operator(smoothed))
    residual = forcing - apply_operator(smoothed)
    partial_value = restrict_blocks(residual, aggregate)
    coarse_rhs = lax.psum(partial_value, ("grp", "mem"))
    all_factors = lax.all_gather(factors, "mem", axis=0, tiled=True)
    coarse_fix = solve_blocks(coarse_rhs, all_factors)
    lifted = prolong_blocks(coarse_fix, aggregate, jnp.ones(aggregate.shape, jnp.float32))
    correction = lifted - weight * apply_operator(lifted)
    solution = smoothed + correction
    for repeat in range(POST):
        solution = solution + weight * (forcing - apply_operator(solution))
    return solution


def solution(mesh):
    placed = (P(None, "grp", "mem", None), P("grp", "mem", None), P("mem", None, None))
    return jax.shard_map(
        shards, mesh=mesh, in_specs=placed, out_specs=P(None, "grp", "mem", None), check_vma=False
    )
```

profile of v0, /device:TPU:8, one launch (start us, length us, event | category | flops | bytes accessed | tf_op | source)
XLA Modules:
  0.0 380.2 jit_solution(7049673006676737177)
XLA Ops:
  14.4 4.7 %collective-permute-done.1 = f32[16,1,16,128]{3,2,1,0:T(8,128)S(1)} collective-permute-done((f32[16,1,16,128]{3,2,1,0:T(8,128)S(1)}, f32[16,1,16,128]{3,2,1,0:T(8,128)S(1)}, u32[]{:S(2)}, u32[]{:S(2)}) %collective-permute-start.1) | collective-permute-done | bytes 131104 | tf_op jit(solution)/shard_map/ppermute | solution.py:20
  19.3 3.4 collective-permute-start.3
  25.6 4.4 %collective-permute-done.2 = f32[16,18,1,128]{3,0,2,1:T(8,128)S(1)} collective-permute-done((f32[16,18,1,128]{3,0,2,1:T(8,128)S(1)}, f32[16,18,1,128]{3,0,2,1:T(8,128)S(1)}, u32[]{:S(2)}, u32[]{:S(2)}) %collective-permute-start.2) | collective-permute-done | bytes 147488 | tf_op jit(solution)/shard_map/ppermute | solution.py:22
  36.7 4.7 %collective-permute-done.5 = f32[16,1,16,128]{3,2,1,0:T(8,128)S(1)} collective-permute-done((f32[16,1,16,128]{3,2,1,0:T(8,128)S(1)}, f32[16,1,16,128]{3,2,1,0:T(8,128)S(1)}, u32[]{:S(2)}, u32[]{:S(2)}) %collective-permute-start.5) | collective-permute-done | bytes 131104 | tf_op jit(solution)/shard_map/ppermute | solution.py:20
  45.9 4.3 %collective-permute-done.6 = f32[16,18,1,128]{3,0,2,1:T(8,128)S(1)} collective-permute-done((f32[16,18,1,128]{3,0,2,1:T(8,128)S(1)}, f32[16,18,1,128]{3,0,2,1:T(8,128)S(1)}, u32[]{:S(2)}, u32[]{:S(2)}) %collective-permute-start.6) | collective-permute-done | bytes 147488 | tf_op jit(solution)/shard_map/ppermute | solution.py:22
  56.8 4.7 %collective-permute-done.9 = f32[16,1,16,128]{3,2,1,0:T(8,128)S(1)} collective-permute-done((f32[16,1,16,128]{3,2,1,0:T(8,128)S(1)}, f32[16,1,16,128]{3,2,1,0:T(8,128)S(1)}, u32[]{:S(2)}, u32[]{:S(2)}) %collective-permute-start.9) | collective-permute-done | bytes 131104 | tf_op jit(solution)/shard_map/ppermute | solution.py:20
  66.0 4.4 %collective-permute-done.10 = f32[16,18,1,128]{3,0,2,1:T(8,128)S(1)} collective-permute-done((f32[16,18,1,128]{3,0,2,1:T(8,128)S(1)}, f32[16,18,1,128]{3,0,2,1:T(8,128)S(1)}, u32[]{:S(2)}, u32[]{:S(2)}) %collective-permute-start.10) | collective-permute-done | bytes 147488 | tf_op jit(solution)/shard_map/ppermute | solution.py:22
  73.4 10.0 %copy.356 = f32[16,16,16,128]{0,3,2,1:T(8,128)} copy(f32[16,16,16,128]{3,2,1,0:T(8,128)} %fusion.31) | data formatting | bytes 4194304 | tf_op jit(solution)/shard_map/sub | solution.py:80
  83.4 9.4 %reduce_sum.9 = f32[16,4,4,32]{0,3,2,1:T(8,128)S(1)} reduce(f32[16,4,4,4,4,32,4]{0,6,5,4,3,2,1:T(4,128)} %bitcast.23, f32[]{:T(128)} %constant.11.clone.1), dimensions={2,4,6}, to_apply=%region_0.0 | reduce | flops 516096 | bytes 2129924 | tf_op jit(solution)/shard_map/reduce_sum | solution.py:49
  92.8 4.4 %scatter_custom_fusion = f32[8192,16]{1,0:T(8,128)} fusion(s32[512]{0:T(512)S(1)} %reshape.77, f32[512,16]{1,0:T(8,128)S(1)} %bitcast.27, f32[]{:T(128)} %constant.11.clone.1), kind=kCustom, calls=%fused_computation.102 | custom fusion | flops 8192 | bytes 524292 | tf_op jit(solution)/shard_map/scatter-add | solution.py:52
  97.2 3.5 copy.358
  101.4 166.7 %all-reduce.14.cloned.1.call-done = f32[16,64,128]{2,0,1:T(8,128)} async-done(((f32[16,64,128]{2,0,1:T(8,128)}), f32[16,64,128]{2,0,1:T(8,128)}) %all-reduce.14.cloned.1.call-update) | async-done | bytes 524304 | tf_op jit(solution)/shard_map/psum | solution.py:82
  268.1 8.6 %convolution_bitcast_fusion.1 = f32[16,64,128]{2,0,1:T(8,128)S(1)} fusion(f32[16,64,128]{2,0,1:T(8,128)} %all-reduce.14.cloned.1.call-done, f32[64,128,128]{2,1,0:T(8,128)} %all-gather.2.cloned.1.call-done), kind=kOutput, calls=%fused_computation.105 | convolution fusion | flops 201326592 | bytes 5242880 | tf_op jit(solution)/shard_map/kbj,bij->kbi/dot_general | solution.py:70
  276.8 3.8 convolution_bitcast_fusion
  286.5 3.9 %broadcast_in_dim.21 = f32[16,4,4,4,4,32,4]{0,6,5,4,3,2,1:T(4,128)S(1)} broadcast(f32[16,4,4,32]{0,3,2,1:T(8,128)S(1)} %broadcast_select_fusion), dimensions={0,1,3,5} | broadcast | bytes 2129920 | tf_op jit(solution)/shard_map/broadcast_in_dim | solution.py:61
  290.4 5.7 %copy-done = f32[16,4,4,4,4,32,4]{0,6,5,4,3,2,1:T(4,128)} copy-done((f32[16,4,4,4,4,32,4]{0,6,5,4,3,2,1:T(4,128)}, f32[16,4,4,4,4,32,4]{0,6,5,4,3,2,1:T(4,128)S(1)}, u32[]{:S(2)}) %copy-start) | copy-done | bytes 2097176
  303.5 11.0 %copy.373 = f32[16,16,16,128]{3,2,1,0:T(8,128)} copy(f32[16,16,16,128]{0,3,2,1:T(8,128)} %bitcast.22) | data formatting | bytes 4194304 | tf_op jit(solution)/shard_map/reshape | solution.py:62
  316.5 3.4 collective-permute-start.15
  323.5 4.0 %collective-permute-done.14 = f32[16,18,1,128]{3,0,2,1:T(8,128)S(1)} collective-permute-done((f32[16,18,1,128]{3,0,2,1:T(8,128)S(1)}, f32[16,18,1,128]{3,0,2,1:T(8,128)S(1)}, u32[]{:S(2)}, u32[]{:S(2)}) %collective-permute-start.14) | collective-permute-done | bytes 147488 | tf_op jit(solution)/shard_map/ppermute | solution.py:22
  329.6 3.8 %collective-permute-start.16 = (f32[16,1,16,128]{3,2,1,0:T(8,128)S(1)}, f32[16,1,16,128]{3,2,1,0:T(8,128)S(1)}, u32[]{:S(2)}, u32[]{:S(2)}) collective-permute-start(f32[16,1,16,128]{3,2,1,0:T(8,128)S(1)} %get-tuple-element.26), channel_id=1, source_target_pairs={{2,0},{4,2},{6,4},{8,6},{10,8},{12,10},{14,12},{16,14},{18,16},{20... | collective-permute-start | bytes 393224 | tf_op jit(solution)/shard_map/ppermute | solution.py:22
  336.0 4.7 %collective-permute-done.17 = f32[16,1,16,128]{3,2,1,0:T(8,128)S(1)} collective-permute-done((f32[16,1,16,128]{3,2,1,0:T(8,128)S(1)}, f32[16,1,16,128]{3,2,1,0:T(8,128)S(1)}, u32[]{:S(2)}, u32[]{:S(2)}) %collective-permute-start.17) | collective-permute-done | bytes 131104 | tf_op jit(solution)/shard_map/ppermute | solution.py:20
  345.1 4.4 %collective-permute-done.18 = f32[16,18,1,128]{3,0,2,1:T(8,128)S(1)} collective-permute-done((f32[16,18,1,128]{3,0,2,1:T(8,128)S(1)}, f32[16,18,1,128]{3,0,2,1:T(8,128)S(1)}, u32[]{:S(2)}, u32[]{:S(2)}) %collective-permute-start.18) | collective-permute-done | bytes 147488 | tf_op jit(solution)/shard_map/ppermute | solution.py:22
  356.2 4.7 %collective-permute-done.21 = f32[16,1,16,128]{3,2,1,0:T(8,128)S(1)} collective-permute-done((f32[16,1,16,128]{3,2,1,0:T(8,128)S(1)}, f32[16,1,16,128]{3,2,1,0:T(8,128)S(1)}, u32[]{:S(2)}, u32[]{:S(2)}) %collective-permute-start.21) | collective-permute-done | bytes 131104 | tf_op jit(solution)/shard_map/ppermute | solution.py:20
  365.4 4.3 %collective-permute-done.22 = f32[16,18,1,128]{3,0,2,1:T(8,128)S(1)} collective-permute-done((f32[16,18,1,128]{3,0,2,1:T(8,128)S(1)}, f32[16,18,1,128]{3,0,2,1:T(8,128)S(1)}, u32[]{:S(2)}, u32[]{:S(2)}) %collective-permute-start.22) | collective-permute-done | bytes 147488 | tf_op jit(solution)/shard_map/ppermute | solution.py:22
  (112 shorter events, 78.0 us)
Async XLA Ops:
  7.4 260.8 %all-reduce.14.cloned.1.call-start = ((), (), s32[]{:S(2)}) async-start(), calls=%async_computation | async-start | bytes 1048576 | tf_op jit(solution)/shard_map/psum | solution.py:82
  9.2 5.2 %collective-permute-start = (f32[16,1,16,128]{3,2,1,0:T(8,128)S(1)}, f32[16,1,16,128]{3,2,1,0:T(8,128)S(1)}, u32[]{:S(2)}, u32[]{:S(2)}) collective-permute-start(f32[16,1,16,128]{3,2,1,0:T(8,128)S(1)} %get-tuple-element.40), channel_id=1, source_target_pairs={{2,0},{4,2},{6,4},{8,6},{10,8},{12,10},{14,12},{16,14},{18,16},{20... | collective-permute-start | bytes 393224 | tf_op jit(solution)/shard_map/ppermute | solution.py:22
  11.9 7.2 %collective-permute-start.1 = (f32[16,1,16,128]{3,2,1,0:T(8,128)S(1)}, f32[16,1,16,128]{3,2,1,0:T(8,128)S(1)}, u32[]{:S(2)}, u32[]{:S(2)}) collective-permute-start(f32[16,1,16,128]{3,2,1,0:T(8,128)S(1)} %get-tuple-element.39), channel_id=1, source_target_pairs={{0,2},{2,4},{4,6},{6,8},{8,10},{10,12},{12,14},{14,16},{16,18},{18... | collective-permute-start | bytes 393224 | tf_op jit(solution)/shard_map/ppermute | solution.py:20
  19.3 6.1 %collective-permute-start.3 = (f32[16,18,1,128]{3,0,2,1:T(8,128)S(1)}, f32[16,18,1,128]{3,0,2,1:T(8,128)S(1)}, u32[]{:S(2)}, u32[]{:S(2)}) collective-permute-start(f32[16,18,1,128]{3,0,2,1:T(8,128)S(1)} %copy.346), channel_id=1, source_target_pairs={{0,1},{2,3},{4,5},{6,7},{8,9},{10,11},{12,13},{14,15},{16,17},{18,... | collective-permute-start | bytes 442376 | tf_op jit(solution)/shard_map/ppermute | solution.py:20
  22.8 7.2 %collective-permute-start.2 = (f32[16,18,1,128]{3,0,2,1:T(8,128)S(1)}, f32[16,18,1,128]{3,0,2,1:T(8,128)S(1)}, u32[]{:S(2)}, u32[]{:S(2)}) collective-permute-start(f32[16,18,1,128]{3,0,2,1:T(8,128)S(1)} %copy.344), channel_id=1, source_target_pairs={{1,0},{3,2},{5,4},{7,6},{9,8},{11,10},{13,12},{15,14},{17,16},{19,... | collective-permute-start | bytes 442376 | tf_op jit(solution)/shard_map/ppermute | solution.py:22
  32.2 4.4 %collective-permute-start.4 = (f32[16,1,16,128]{3,2,1,0:T(8,128)S(1)}, f32[16,1,16,128]{3,2,1,0:T(8,128)S(1)}, u32[]{:S(2)}, u32[]{:S(2)}) collective-permute-start(f32[16,1,16,128]{3,2,1,0:T(8,128)S(1)} %get-tuple-element.36), channel_id=1, source_target_pairs={{2,0},{4,2},{6,4},{8,6},{10,8},{12,10},{14,12},{16,14},{18,16},{20... | collective-permute-start | bytes 393224 | tf_op jit(solution)/shard_map/ppermute | solution.py:22
  34.2 7.2 %collective-permute-start.5 = (f32[16,1,16,128]{3,2,1,0:T(8,128)S(1)}, f32[16,1,16,128]{3,2,1,0:T(8,128)S(1)}, u32[]{:S(2)}, u32[]{:S(2)}) collective-permute-start(f32[16,1,16,128]{3,2,1,0:T(8,128)S(1)} %get-tuple-element.35), channel_id=1, source_target_pairs={{0,2},{2,4},{4,6},{6,8},{8,10},{10,12},{12,14},{14,16},{16,18},{18... | collective-permute-start | bytes 393224 | tf_op jit(solution)/shard_map/ppermute | solution.py:20
  41.6 4.1 %collective-permute-start.7 = (f32[16,18,1,128]{3,0,2,1:T(8,128)S(1)}, f32[16,18,1,128]{3,0,2,1:T(8,128)S(1)}, u32[]{:S(2)}, u32[]{:S(2)}) collective-permute-start(f32[16,18,1,128]{3,0,2,1:T(8,128)S(1)} %copy.350), channel_id=1, source_target_pairs={{0,1},{2,3},{4,5},{6,7},{8,9},{10,11},{12,13},{14,15},{16,17},{18,... | collective-permute-start | bytes 442376 | tf_op jit(solution)/shard_map/ppermute | solution.py:20
  43.1 7.0 %collective-permute-start.6 = (f32[16,18,1,128]{3,0,2,1:T(8,128)S(1)}, f32[16,18,1,128]{3,0,2,1:T(8,128)S(1)}, u32[]{:S(2)}, u32[]{:S(2)}) collective-permute-start(f32[16,18,1,128]{3,0,2,1:T(8,128)S(1)} %copy.348), channel_id=1, source_target_pairs={{1,0},{3,2},{5,4},{7,6},{9,8},{11,10},{13,12},{15,14},{17,16},{19,... | collective-permute-start | bytes 442376 | tf_op jit(solution)/shard_map/ppermute | solution.py:22
  52.3 4.4 %collective-permute-start.8 = (f32[16,1,16,128]{3,2,1,0:T(8,128)S(1)}, f32[16,1,16,128]{3,2,1,0:T(8,128)S(1)}, u32[]{:S(2)}, u32[]{:S(2)}) collective-permute-start(f32[16,1,16,128]{3,2,1,0:T(8,128)S(1)} %get-tuple-element.32), channel_id=1, source_target_pairs={{2,0},{4,2},{6,4},{8,6},{10,8},{12,10},{14,12},{16,14},{18,16},{20... | collective-permute-start | bytes 393224 | tf_op jit(solution)/shard_map/ppermute | solution.py:22
  54.3 7.2 %collective-permute-start.9 = (f32[16,1,16,128]{3,2,1,0:T(8,128)S(1)}, f32[16,1,16,128]{3,2,1,0:T(8,128)S(1)}, u32[]{:S(2)}, u32[]{:S(2)}) collective-permute-start(f32[16,1,16,128]{3,2,1,0:T(8,128)S(1)} %get-tuple-element.31), channel_id=1, source_target_pairs={{0,2},{2,4},{4,6},{6,8},{8,10},{10,12},{12,14},{14,16},{16,18},{18... | collective-permute-start | bytes 393224 | tf_op jit(solution)/shard_map/ppermute | solution.py:20
  61.7 4.1 %collective-permute-start.11 = (f32[16,18,1,128]{3,0,2,1:T(8,128)S(1)}, f32[16,18,1,128]{3,0,2,1:T(8,128)S(1)}, u32[]{:S(2)}, u32[]{:S(2)}) collective-permute-start(f32[16,18,1,128]{3,0,2,1:T(8,128)S(1)} %copy.354), channel_id=1, source_target_pairs={{0,1},{2,3},{4,5},{6,7},{8,9},{10,11},{12,13},{14,15},{16,17},{18,... | collective-permute-start | bytes 442376 | tf_op jit(solution)/shard_map/ppermute | solution.py:20
  63.2 7.2 %collective-permute-start.10 = (f32[16,18,1,128]{3,0,2,1:T(8,128)S(1)}, f32[16,18,1,128]{3,0,2,1:T(8,128)S(1)}, u32[]{:S(2)}, u32[]{:S(2)}) collective-permute-start(f32[16,18,1,128]{3,0,2,1:T(8,128)S(1)} %copy.352), channel_id=1, source_target_pairs={{1,0},{3,2},{5,4},{7,6},{9,8},{11,10},{13,12},{15,14},{17,16},{19,... | collective-permute-start | bytes 442376 | tf_op jit(solution)/shard_map/ppermute | solution.py:22
  100.7 167.4 %all-gather.2.cloned.1.call-start = ((), (), s32[]{:S(2)}) async-start(), calls=%async_computation.1 | async-start | bytes 6291456 | tf_op jit(solution)/shard_map/all_gather | solution.py:83
  298.9 15.7 %collective-permute-start.12 = (f32[16,1,16,128]{3,2,1,0:T(8,128)S(1)}, f32[16,1,16,128]{3,2,1,0:T(8,128)S(1)}, u32[]{:S(2)}, u32[]{:S(2)}) collective-permute-start(f32[16,1,16,128]{3,2,1,0:T(8,128)S(1)} %copy.362), channel_id=1, source_target_pairs={{2,0},{4,2},{6,4},{8,6},{10,8},{12,10},{14,12},{16,14},{18,16},{20... | collective-permute-start | bytes 393224 | tf_op jit(solution)/shard_map/ppermute | solution.py:22
  301.2 13.3 %collective-permute-start.13 = (f32[16,1,16,128]{3,2,1,0:T(8,128)S(1)}, f32[16,1,16,128]{3,2,1,0:T(8,128)S(1)}, u32[]{:S(2)}, u32[]{:S(2)}) collective-permute-start(f32[16,1,16,128]{3,2,1,0:T(8,128)S(1)} %copy.364), channel_id=1, source_target_pairs={{0,2},{2,4},{4,6},{6,8},{8,10},{10,12},{12,14},{14,16},{16,18},{18... | collective-permute-start | bytes 393224 | tf_op jit(solution)/shard_map/ppermute | solution.py:20
  316.5 6.8 %collective-permute-start.15 = (f32[16,18,1,128]{3,0,2,1:T(8,128)S(1)}, f32[16,18,1,128]{3,0,2,1:T(8,128)S(1)}, u32[]{:S(2)}, u32[]{:S(2)}) collective-permute-start(f32[16,18,1,128]{3,0,2,1:T(8,128)S(1)} %copy.369), channel_id=1, source_target_pairs={{0,1},{2,3},{4,5},{6,7},{8,9},{10,11},{12,13},{14,15},{16,17},{18,... | collective-permute-start | bytes 442376 | tf_op jit(solution)/shard_map/ppermute | solution.py:20
  319.9 7.5 %collective-permute-start.14 = (f32[16,18,1,128]{3,0,2,1:T(8,128)S(1)}, f32[16,18,1,128]{3,0,2,1:T(8,128)S(1)}, u32[]{:S(2)}, u32[]{:S(2)}) collective-permute-start(f32[16,18,1,128]{3,0,2,1:T(8,128)S(1)} %copy.367), channel_id=1, source_target_pairs={{1,0},{3,2},{5,4},{7,6},{9,8},{11,10},{13,12},{15,14},{17,16},{19,... | collective-permute-start | bytes 442376 | tf_op jit(solution)/shard_map/ppermute | solution.py:22
  329.6 6.3 %collective-permute-start.16 = (f32[16,1,16,128]{3,2,1,0:T(8,128)S(1)}, f32[16,1,16,128]{3,2,1,0:T(8,128)S(1)}, u32[]{:S(2)}, u32[]{:S(2)}) collective-permute-start(f32[16,1,16,128]{3,2,1,0:T(8,128)S(1)} %get-tuple-element.26), channel_id=1, source_target_pairs={{2,0},{4,2},{6,4},{8,6},{10,8},{12,10},{14,12},{16,14},{18,16},{20... | collective-permute-start | bytes 393224 | tf_op jit(solution)/shard_map/ppermute | solution.py:22
  333.5 7.2 %collective-permute-start.17 = (f32[16,1,16,128]{3,2,1,0:T(8,128)S(1)}, f32[16,1,16,128]{3,2,1,0:T(8,128)S(1)}, u32[]{:S(2)}, u32[]{:S(2)}) collective-permute-start(f32[16,1,16,128]{3,2,1,0:T(8,128)S(1)} %get-tuple-element.25), channel_id=1, source_target_pairs={{0,2},{2,4},{4,6},{6,8},{8,10},{10,12},{12,14},{14,16},{16,18},{18... | collective-permute-start | bytes 393224 | tf_op jit(solution)/shard_map/ppermute | solution.py:20
  342.4 7.2 %collective-permute-start.18 = (f32[16,18,1,128]{3,0,2,1:T(8,128)S(1)}, f32[16,18,1,128]{3,0,2,1:T(8,128)S(1)}, u32[]{:S(2)}, u32[]{:S(2)}) collective-permute-start(f32[16,18,1,128]{3,0,2,1:T(8,128)S(1)} %copy.374), channel_id=1, source_target_pairs={{1,0},{3,2},{5,4},{7,6},{9,8},{11,10},{13,12},{15,14},{17,16},{19,... | collective-permute-start | bytes 442376 | tf_op jit(solution)/shard_map/ppermute | solution.py:22
  351.8 4.4 %collective-permute-start.20 = (f32[16,1,16,128]{3,2,1,0:T(8,128)S(1)}, f32[16,1,16,128]{3,2,1,0:T(8,128)S(1)}, u32[]{:S(2)}, u32[]{:S(2)}) collective-permute-start(f32[16,1,16,128]{3,2,1,0:T(8,128)S(1)} %get-tuple-element.22), channel_id=1, source_target_pairs={{2,0},{4,2},{6,4},{8,6},{10,8},{12,10},{14,12},{16,14},{18,16},{20... | collective-permute-start | bytes 393224 | tf_op jit(solution)/shard_map/ppermute | solution.py:22
  353.7 7.2 %collective-permute-start.21 = (f32[16,1,16,128]{3,2,1,0:T(8,128)S(1)}, f32[16,1,16,128]{3,2,1,0:T(8,128)S(1)}, u32[]{:S(2)}, u32[]{:S(2)}) collective-permute-start(f32[16,1,16,128]{3,2,1,0:T(8,128)S(1)} %get-tuple-element.21), channel_id=1, source_target_pairs={{0,2},{2,4},{4,6},{6,8},{8,10},{10,12},{12,14},{14,16},{16,18},{18... | collective-permute-start | bytes 393224 | tf_op jit(solution)/shard_map/ppermute | solution.py:20
  362.6 7.0 %collective-permute-start.22 = (f32[16,18,1,128]{3,0,2,1:T(8,128)S(1)}, f32[16,18,1,128]{3,0,2,1:T(8,128)S(1)}, u32[]{:S(2)}, u32[]{:S(2)}) collective-permute-start(f32[16,18,1,128]{3,0,2,1:T(8,128)S(1)} %copy.378), channel_id=1, source_target_pairs={{1,0},{3,2},{5,4},{7,6},{9,8},{11,10},{13,12},{15,14},{17,16},{19,... | collective-permute-start | bytes 442376 | tf_op jit(solution)/shard_map/ppermute | solution.py:22
  (9 other events, 57.8 us)
Sparse Core Ops, SparseCore 0:
  100.8 167.2 all-reduce.13
Sparse Core Ops, SparseCore 1:
  102.7 56.0 all-gather.1
where the time goes:
time: 381 us; the launch traced here: 380 us
  waiting for transfers between devices  221 us (58%)
  local copies, waits for them, and re-layouts  49.7 us (13%)
  starting transfers between devices  48.9 us (13%)
  other arithmetic  32.7 us (9%)
  between operations  15.5 us (4%)
  matrix products  12.4 us (3%)
    psum x1, waiting for transfers between devices, shards(): coarse_rhs = lax.psum(partial_value, ('grp', 'mem'))  167 us
    ppermute x12, waiting for transfers between devices, with_halo(): lax.ppermute(tail, axis, [(i, (i + 1) % count) for i in range(ends)])  27 us
    ppermute x12, waiting for transfers between devices, with_halo(): lax.ppermute(head, axis, [((i + 1) % count, i) for i in range(ends)])  27 us
    ppermute x12, starting transfers between devices, with_halo(): lax.ppermute(tail, axis, [(i, (i + 1) % count) for i in range(ends)])  26.1 us
    ppermute x12, starting transfers between devices, with_halo(): lax.ppermute(head, axis, [((i + 1) % count, i) for i in range(ends)])  22.7 us
    reshape x1, local copies, waits for them, and re-layouts, prolong_blocks(): return spread.reshape(sides, blk_x * 4, blk_y * 4, blk_z * 4)  11 us
    sub x1, local copies, waits for them, and re-layouts, shards(): residual = forcing - apply_operator(smoothed)  10 us
    reduce_sum x1, other arithmetic, restrict_blocks(): means = residual.reshape(sides, blk_x, 4, blk_y, 4, blk_z, 4).mean(axis=(...  9.37 us
  transfers between devices with their start and end apart: 26, of which 22 were waited for; matrix products, arithmetic and copies ran while one was open for 4% of the time, Pallas kernels for 0%

commit v1 on v0

--- a/solution.py
+++ b/solution.py
@@ -79,7 +79,7 @@
         smoothed = smoothed + weight * (forcing - apply_operator(smoothed))
     residual = forcing - apply_operator(smoothed)
     partial_value = restrict_blocks(residual, aggregate)
-    coarse_rhs = lax.psum(partial_value, ("grp", "mem"))
+    coarse_rhs = lax.psum(lax.psum(partial_value, "mem"), "grp")
     all_factors = lax.all_gather(factors, "mem", axis=0, tiled=True)
     coarse_fix = solve_blocks(coarse_rhs, all_factors)
     lifted = prolong_blocks(coarse_fix, aggregate, jnp.ones(aggregate.shape, jnp.float32))

time: 381 us -> 468 us (1.23)
  waiting for transfers between devices: 221 us -> 311 us
    all_gather x1, waiting for transfers between devices: 0.01 us -> 57.4 us  [shards(): all_factors = lax.all_gather(factors, 'mem', axis=0, tiled=True)]
    psum x1 -> x2, waiting for transfers between devices: 167 us -> 199 us  [shards(): coarse_rhs = lax.psum(lax.psum(partial_value, 'mem'), 'grp')]
  transfers between devices with their start and end apart: 26 -> 27, of which waited for: 22 -> 24; matrix products, arithmetic and copies ran while one was open for 4% -> 4% of each run, Pallas kernels for 0% -> 0%
where the time goes in v1:
time: 468 us; the launch traced here: 467 us
  waiting for transfers between devices  311 us (66%)
  local copies, waits for them, and re-layouts  49.7 us (11%)
  starting transfers between devices  47.7 us (10%)
  other arithmetic  32.6 us (7%)
  between operations  13.7 us (3%)
  matrix products  12.4 us (3%)
    psum x2, waiting for transfers between devices, shards(): coarse_rhs = lax.psum(lax.psum(partial_value, 'mem'), 'grp')  199 us
    all_gather x1, waiting for transfers between devices, shards(): all_factors = lax.all_gather(factors, 'mem', axis=0, tiled=True)  57.4 us
    ppermute x12, waiting for transfers between devices, with_halo(): lax.ppermute(tail, axis, [(i, (i + 1) % count) for i in range(ends)])  27.7 us
    ppermute x12, waiting for transfers between devices, with_halo(): lax.ppermute(head, axis, [((i + 1) % count, i) for i in range(ends)])  27 us
    ppermute x12, starting transfers between devices, with_halo(): lax.ppermute(tail, axis, [(i, (i + 1) % count) for i in range(ends)])  25 us
    ppermute x12, starting transfers between devices, with_halo(): lax.ppermute(head, axis, [((i + 1) % count, i) for i in range(ends)])  22.4 us
    reshape x1, local copies, waits for them, and re-layouts, prolong_blocks(): return spread.reshape(sides, blk_x * 4, blk_y * 4, blk_z * 4)  11 us
    sub x1, local copies, waits for them, and re-layouts, shards(): residual = forcing - apply_operator(smoothed)  10 us
  transfers between devices with their start and end apart: 27, of which 24 were waited for; matrix products, arithmetic and copies ran while one was open for 4% of the time, Pallas kernels for 0%

profile of v1, /device:TPU:8, one launch (start us, length us, event | category | flops | bytes accessed | tf_op | source)
XLA Modules:
  0.0 467.4 jit_solution(8844465992967161503)
XLA Ops:
  13.6 4.7 %collective-permute-done.1 = f32[16,1,16,128]{3,2,1,0:T(8,128)S(1)} collective-permute-done((f32[16,1,16,128]{3,2,1,0:T(8,128)S(1)}, f32[16,1,16,128]{3,2,1,0:T(8,128)S(1)}, u32[]{:S(2)}, u32[]{:S(2)}) %collective-permute-start.1) | collective-permute-done | bytes 131104 | tf_op jit(solution)/shard_map/ppermute | solution.py:20
  18.5 3.4 collective-permute-start.3
  24.8 4.4 collective-permute-done.2
  35.7 4.7 %collective-permute-done.5 = f32[16,1,16,128]{3,2,1,0:T(8,128)S(1)} collective-permute-done((f32[16,1,16,128]{3,2,1,0:T(8,128)S(1)}, f32[16,1,16,128]{3,2,1,0:T(8,128)S(1)}, u32[]{:S(2)}, u32[]{:S(2)}) %collective-permute-start.5) | collective-permute-done | bytes 131104 | tf_op jit(solution)/shard_map/ppermute | solution.py:20
  44.9 4.3 collective-permute-done.6
  55.9 4.7 collective-permute-done.9
  65.1 4.4 collective-permute-done.10
  72.5 10.0 %copy.356 = f32[16,16,16,128]{0,3,2,1:T(8,128)} copy(f32[16,16,16,128]{3,2,1,0:T(8,128)} %fusion.31) | data formatting | bytes 4194304 | tf_op jit(solution)/shard_map/sub | solution.py:80
  82.5 9.4 %reduce_sum.9 = f32[16,4,4,32]{0,3,2,1:T(8,128)S(1)} reduce(f32[16,4,4,4,4,32,4]{0,6,5,4,3,2,1:T(4,128)} %bitcast.22, f32[]{:T(128)} %constant.11.clone.1), dimensions={2,4,6}, to_apply=%region_0.0 | reduce | flops 516096 | bytes 2129924 | tf_op jit(solution)/shard_map/reduce_sum | solution.py:49
  91.9 4.5 scatter_custom_fusion
  96.4 107.3 %all-reduce.15.cloned.1.call-done = f32[16,8192]{0,1:T(8,128)} async-done(((f32[16,8192]{0,1:T(8,128)}), f32[16,8192]{0,1:T(8,128)}) %all-reduce.15.cloned.1.call-update) | async-done | bytes 524304 | tf_op jit(solution)/shard_map/psum | solution.py:82
  203.7 3.5 copy.358
  208.1 91.3 %all-reduce.17.cloned.1.call-done = f32[16,64,128]{2,0,1:T(8,128)} async-done(((f32[16,64,128]{2,0,1:T(8,128)}), f32[16,64,128]{2,0,1:T(8,128)}) %all-reduce.17.cloned.1.call-update) | async-done | bytes 524304 | tf_op jit(solution)/shard_map/psum | solution.py:82
  299.4 57.4 %all-gather.2.cloned.1.call-done = f32[64,128,128]{2,1,0:T(8,128)} async-done(((f32[32,128,128]{2,1,0:T(8,128)}), f32[64,128,128]{2,1,0:T(8,128)}) %all-gather.2.cloned.1.call-update) | async-done | bytes 4194320 | tf_op jit(solution)/shard_map/all_gather | solution.py:83
  356.8 8.6 %convolution_bitcast_fusion.1 = f32[16,64,128]{2,0,1:T(8,128)S(1)} fusion(f32[16,64,128]{2,0,1:T(8,128)} %all-reduce.17.cloned.1.call-done, f32[64,128,128]{2,1,0:T(8,128)} %all-gather.2.cloned.1.call-done), kind=kOutput, calls=%fused_computation.105 | convolution fusion | flops 201326592 | bytes 5242880 | tf_op jit(solution)/shard_map/kbj,bij->kbi/dot_general | solution.py:70
  365.5 3.8 convolution_bitcast_fusion
  375.2 3.9 broadcast_in_dim.21
  379.1 5.7 %copy-done = f32[16,4,4,4,4,32,4]{0,6,5,4,3,2,1:T(4,128)} copy-done((f32[16,4,4,4,4,32,4]{0,6,5,4,3,2,1:T(4,128)}, f32[16,4,4,4,4,32,4]{0,6,5,4,3,2,1:T(4,128)S(1)}, u32[]{:S(2)}) %copy-start) | copy-done | bytes 2097176
  392.5 11.0 %copy.373 = f32[16,16,16,128]{3,2,1,0:T(8,128)} copy(f32[16,16,16,128]{0,3,2,1:T(8,128)} %bitcast.21) | data formatting | bytes 4194304 | tf_op jit(solution)/shard_map/reshape | solution.py:62
  412.2 4.0 collective-permute-done.14
  423.8 4.7 %collective-permute-done.17 = f32[16,1,16,128]{3,2,1,0:T(8,128)S(1)} collective-permute-done((f32[16,1,16,128]{3,2,1,0:T(8,128)S(1)}, f32[16,1,16,128]{3,2,1,0:T(8,128)S(1)}, u32[]{:S(2)}, u32[]{:S(2)}) %collective-permute-start.17) | collective-permute-done | bytes 131104 | tf_op jit(solution)/shard_map/ppermute | solution.py:20
  433.3 4.4 collective-permute-done.18
  444.3 4.7 %collective-permute-done.21 = f32[16,1,16,128]{3,2,1,0:T(8,128)S(1)} collective-permute-done((f32[16,1,16,128]{3,2,1,0:T(8,128)S(1)}, f32[16,1,16,128]{3,2,1,0:T(8,128)S(1)}, u32[]{:S(2)}, u32[]{:S(2)}) %collective-permute-start.21) | collective-permute-done | bytes 131104 | tf_op jit(solution)/shard_map/ppermute | solution.py:20
  453.5 4.3 collective-permute-done.22
  (115 shorter events, 84.7 us)
Async XLA Ops:
  6.5 197.2 %all-reduce.15.cloned.1.call-start = ((), (), s32[]{:S(2)}) async-start(), calls=%async_computation | async-start | bytes 8388608 | tf_op jit(solution)/shard_map/psum | solution.py:82
  8.4 5.2 %collective-permute-start = (f32[16,1,16,128]{3,2,1,0:T(8,128)S(1)}, f32[16,1,16,128]{3,2,1,0:T(8,128)S(1)}, u32[]{:S(2)}, u32[]{:S(2)}) collective-permute-start(f32[16,1,16,128]{3,2,1,0:T(8,128)S(1)} %get-tuple-element.40), channel_id=1, source_target_pairs={{2,0},{4,2},{6,4},{8,6},{10,8},{12,10},{14,12},{16,14},{18,16},{20... | collective-permute-start | bytes 393224 | tf_op jit(solution)/shard_map/ppermute | solution.py:22
  11.1 7.2 %collective-permute-start.1 = (f32[16,1,16,128]{3,2,1,0:T(8,128)S(1)}, f32[16,1,16,128]{3,2,1,0:T(8,128)S(1)}, u32[]{:S(2)}, u32[]{:S(2)}) collective-permute-start(f32[16,1,16,128]{3,2,1,0:T(8,128)S(1)} %get-tuple-element.39), channel_id=1, source_target_pairs={{0,2},{2,4},{4,6},{6,8},{8,10},{10,12},{12,14},{14,16},{16,18},{18... | collective-permute-start | bytes 393224 | tf_op jit(solution)/shard_map/ppermute | solution.py:20
  18.5 6.1 %collective-permute-start.3 = (f32[16,18,1,128]{3,0,2,1:T(8,128)S(1)}, f32[16,18,1,128]{3,0,2,1:T(8,128)S(1)}, u32[]{:S(2)}, u32[]{:S(2)}) collective-permute-start(f32[16,18,1,128]{3,0,2,1:T(8,128)S(1)} %copy.346), channel_id=1, source_target_pairs={{0,1},{2,3},{4,5},{6,7},{8,9},{10,11},{12,13},{14,15},{16,17},{18,... | collective-permute-start | bytes 442376 | tf_op jit(solution)/shard_map/ppermute | solution.py:20
  22.0 7.2 %collective-permute-start.2 = (f32[16,18,1,128]{3,0,2,1:T(8,128)S(1)}, f32[16,18,1,128]{3,0,2,1:T(8,128)S(1)}, u32[]{:S(2)}, u32[]{:S(2)}) collective-permute-start(f32[16,18,1,128]{3,0,2,1:T(8,128)S(1)} %copy.344), channel_id=1, source_target_pairs={{1,0},{3,2},{5,4},{7,6},{9,8},{11,10},{13,12},{15,14},{17,16},{19,... | collective-permute-start | bytes 442376 | tf_op jit(solution)/shard_map/ppermute | solution.py:22
  31.3 4.4 collective-permute-start.4
  33.2 7.2 %collective-permute-start.5 = (f32[16,1,16,128]{3,2,1,0:T(8,128)S(1)}, f32[16,1,16,128]{3,2,1,0:T(8,128)S(1)}, u32[]{:S(2)}, u32[]{:S(2)}) collective-permute-start(f32[16,1,16,128]{3,2,1,0:T(8,128)S(1)} %get-tuple-element.35), channel_id=1, source_target_pairs={{0,2},{2,4},{4,6},{6,8},{8,10},{10,12},{12,14},{14,16},{16,18},{18... | collective-permute-start | bytes 393224 | tf_op jit(solution)/shard_map/ppermute | solution.py:20
  42.2 7.0 %collective-permute-start.6 = (f32[16,18,1,128]{3,0,2,1:T(8,128)S(1)}, f32[16,18,1,128]{3,0,2,1:T(8,128)S(1)}, u32[]{:S(2)}, u32[]{:S(2)}) collective-permute-start(f32[16,18,1,128]{3,0,2,1:T(8,128)S(1)} %copy.348), channel_id=1, source_target_pairs={{1,0},{3,2},{5,4},{7,6},{9,8},{11,10},{13,12},{15,14},{17,16},{19,... | collective-permute-start | bytes 442376 | tf_op jit(solution)/shard_map/ppermute | solution.py:22
  51.4 4.4 collective-permute-start.8
  53.4 7.2 %collective-permute-start.9 = (f32[16,1,16,128]{3,2,1,0:T(8,128)S(1)}, f32[16,1,16,128]{3,2,1,0:T(8,128)S(1)}, u32[]{:S(2)}, u32[]{:S(2)}) collective-permute-start(f32[16,1,16,128]{3,2,1,0:T(8,128)S(1)} %get-tuple-element.31), channel_id=1, source_target_pairs={{0,2},{2,4},{4,6},{6,8},{8,10},{10,12},{12,14},{14,16},{16,18},{18... | collective-permute-start | bytes 393224 | tf_op jit(solution)/shard_map/ppermute | solution.py:20
  62.3 7.2 %collective-permute-start.10 = (f32[16,18,1,128]{3,0,2,1:T(8,128)S(1)}, f32[16,18,1,128]{3,0,2,1:T(8,128)S(1)}, u32[]{:S(2)}, u32[]{:S(2)}) collective-permute-start(f32[16,18,1,128]{3,0,2,1:T(8,128)S(1)} %copy.352), channel_id=1, source_target_pairs={{1,0},{3,2},{5,4},{7,6},{9,8},{11,10},{13,12},{15,14},{17,16},{19,... | collective-permute-start | bytes 442376 | tf_op jit(solution)/shard_map/ppermute | solution.py:22
  96.4 203.1 %all-reduce.17.cloned.1.call-start = ((), (), s32[]{:S(2)}) async-start(), calls=%async_computation.1 | async-start | bytes 1048576 | tf_op jit(solution)/shard_map/psum | solution.py:82
  207.2 149.6 %all-gather.2.cloned.1.call-start = ((), (), s32[]{:S(2)}) async-start(), calls=%async_computation.2 | async-start | bytes 6291456 | tf_op jit(solution)/shard_map/all_gather | solution.py:83
  387.6 15.9 %collective-permute-start.12 = (f32[16,1,16,128]{3,2,1,0:T(8,128)S(1)}, f32[16,1,16,128]{3,2,1,0:T(8,128)S(1)}, u32[]{:S(2)}, u32[]{:S(2)}) collective-permute-start(f32[16,1,16,128]{3,2,1,0:T(8,128)S(1)} %copy.362), channel_id=1, source_target_pairs={{2,0},{4,2},{6,4},{8,6},{10,8},{12,10},{14,12},{16,14},{18,16},{20... | collective-permute-start | bytes 393224 | tf_op jit(solution)/shard_map/ppermute | solution.py:22
  390.5 12.9 %collective-permute-start.13 = (f32[16,1,16,128]{3,2,1,0:T(8,128)S(1)}, f32[16,1,16,128]{3,2,1,0:T(8,128)S(1)}, u32[]{:S(2)}, u32[]{:S(2)}) collective-permute-start(f32[16,1,16,128]{3,2,1,0:T(8,128)S(1)} %copy.364), channel_id=1, source_target_pairs={{0,2},{2,4},{4,6},{6,8},{8,10},{10,12},{12,14},{14,16},{16,18},{18... | collective-permute-start | bytes 393224 | tf_op jit(solution)/shard_map/ppermute | solution.py:20
  405.4 6.6 %collective-permute-start.15 = (f32[16,18,1,128]{3,0,2,1:T(8,128)S(1)}, f32[16,18,1,128]{3,0,2,1:T(8,128)S(1)}, u32[]{:S(2)}, u32[]{:S(2)}) collective-permute-start(f32[16,18,1,128]{3,0,2,1:T(8,128)S(1)} %copy.369), channel_id=1, source_target_pairs={{0,1},{2,3},{4,5},{6,7},{8,9},{10,11},{12,13},{14,15},{16,17},{18,... | collective-permute-start | bytes 442376 | tf_op jit(solution)/shard_map/ppermute | solution.py:20
  407.9 8.2 %collective-permute-start.14 = (f32[16,18,1,128]{3,0,2,1:T(8,128)S(1)}, f32[16,18,1,128]{3,0,2,1:T(8,128)S(1)}, u32[]{:S(2)}, u32[]{:S(2)}) collective-permute-start(f32[16,18,1,128]{3,0,2,1:T(8,128)S(1)} %copy.367), channel_id=1, source_target_pairs={{1,0},{3,2},{5,4},{7,6},{9,8},{11,10},{13,12},{15,14},{17,16},{19,... | collective-permute-start | bytes 442376 | tf_op jit(solution)/shard_map/ppermute | solution.py:22
  418.4 5.5 %collective-permute-start.16 = (f32[16,1,16,128]{3,2,1,0:T(8,128)S(1)}, f32[16,1,16,128]{3,2,1,0:T(8,128)S(1)}, u32[]{:S(2)}, u32[]{:S(2)}) collective-permute-start(f32[16,1,16,128]{3,2,1,0:T(8,128)S(1)} %get-tuple-element.26), channel_id=1, source_target_pairs={{2,0},{4,2},{6,4},{8,6},{10,8},{12,10},{14,12},{16,14},{18,16},{20... | collective-permute-start | bytes 393224 | tf_op jit(solution)/shard_map/ppermute | solution.py:22
  421.3 7.2 %collective-permute-start.17 = (f32[16,1,16,128]{3,2,1,0:T(8,128)S(1)}, f32[16,1,16,128]{3,2,1,0:T(8,128)S(1)}, u32[]{:S(2)}, u32[]{:S(2)}) collective-permute-start(f32[16,1,16,128]{3,2,1,0:T(8,128)S(1)} %get-tuple-element.25), channel_id=1, source_target_pairs={{0,2},{2,4},{4,6},{6,8},{8,10},{10,12},{12,14},{14,16},{16,18},{18... | collective-permute-start | bytes 393224 | tf_op jit(solution)/shard_map/ppermute | solution.py:20
  428.7 4.4 collective-permute-start.19
  430.5 7.2 %collective-permute-start.18 = (f32[16,18,1,128]{3,0,2,1:T(8,128)S(1)}, f32[16,18,1,128]{3,0,2,1:T(8,128)S(1)}, u32[]{:S(2)}, u32[]{:S(2)}) collective-permute-start(f32[16,18,1,128]{3,0,2,1:T(8,128)S(1)} %copy.374), channel_id=1, source_target_pairs={{1,0},{3,2},{5,4},{7,6},{9,8},{11,10},{13,12},{15,14},{17,16},{19,... | collective-permute-start | bytes 442376 | tf_op jit(solution)/shard_map/ppermute | solution.py:22
  439.9 4.4 collective-permute-start.20
  441.8 7.2 %collective-permute-start.21 = (f32[16,1,16,128]{3,2,1,0:T(8,128)S(1)}, f32[16,1,16,128]{3,2,1,0:T(8,128)S(1)}, u32[]{:S(2)}, u32[]{:S(2)}) collective-permute-start(f32[16,1,16,128]{3,2,1,0:T(8,128)S(1)} %get-tuple-element.21), channel_id=1, source_target_pairs={{0,2},{2,4},{4,6},{6,8},{8,10},{10,12},{12,14},{14,16},{16,18},{18... | collective-permute-start | bytes 393224 | tf_op jit(solution)/shard_map/ppermute | solution.py:20
  450.7 7.0 %collective-permute-start.22 = (f32[16,18,1,128]{3,0,2,1:T(8,128)S(1)}, f32[16,18,1,128]{3,0,2,1:T(8,128)S(1)}, u32[]{:S(2)}, u32[]{:S(2)}) collective-permute-start(f32[16,18,1,128]{3,0,2,1:T(8,128)S(1)} %copy.378), channel_id=1, source_target_pairs={{1,0},{3,2},{5,4},{7,6},{9,8},{11,10},{13,12},{15,14},{17,16},{19,... | collective-permute-start | bytes 442376 | tf_op jit(solution)/shard_map/ppermute | solution.py:22
  (10 other events, 61.0 us)
Sparse Core Ops, SparseCore 0:
  96.5 107.1 all-reduce.14
  207.4 92.0 all-reduce.16
  301.0 55.8 all-gather.1
